TPU v7x, 256 devices: a whole 4x4x8 slice. The times are simulated.
256 devices in a mesh: seq: 8 (over y, core), vocab: 32 (over z, x).
Axes of the slice: x: 4, y: 4, z: 8, core: 2. Of those that a mesh axis runs over, the one named last changes fastest.
Arguments:
- hidden: bfloat16 [2, 1024, 5120], P(None, 'seq'), may hold values from -128 to 128
- head_weight: bfloat16 [5120, 77824], P('seq', 'vocab'), may hold values from -1 to 1
- ref_logits: bfloat16 [2, 1024, 77824], P(None, 'seq', 'vocab'), may hold values from -320 to 320
- token_ids: int32 [2, 1024], P(None, 'seq'), may hold values from 0 to 77823
- end_pos: int32 [2], replicated, may hold values from 512 to 1023
- loss_mask: int32 [2, 1024], P(None, 'seq'), may hold values 0 or 1
- scores: float32 [2], replicated, may hold values from -8 to 8
Outputs:
- logit_grad: bfloat16 [2, 1024, 77824], P(None, 'seq', 'vocab')
- hidden_grad: bfloat16 [2, 1024, 5120], P(None, 'seq', 'vocab')
- advantages: float32 [2, 1024], P(None, 'seq')
All inputs are finite; a program needn't handle non-finite values. No bound on the sum of `loss_mask` on one device may be relied on, other than what follows from the above.
Results may differ from a plain program's by a relative error of at most 0.0039.
The roundings to bfloat16 on the way count: a program that leaves them out, or rounds other values in their place, can miss the bound.
Values may be sent and summed in bfloat16 or wider, within the bound.
No kernel may reach another device: no remote copies, remote signals or barrier semaphores. Data moves between devices by JAX's collectives and lax.ppermute only.
A program may use at most 128 MiB of HBM per device.

v0:
```python
import jax
import jax.numpy as jnp
from jax import lax
from jax.sharding import PartitionSpec as P


def from_behind(shard, axis, by):
    devices = lax.axis_size(axis)
    pairs = [(i, i + by) for i in range(devices) if 0 <= i + by < devices]
    return lax.ppermute(shard, axis, pairs)


def per_device(hidden, head_weight, ref_logits, token_ids, end_pos, loss_mask, scores):
    batch, segment, width = hidden.shape
    vocab_dev = head_weight.shape[1]
    seq_start = lax.axis_index("seq") * segment
    vocab_start = lax.axis_index("vocab") * vocab_dev
    whole_head = lax.all_gather(head_weight, "seq", axis=0, tiled=True)
    logits = jnp.dot(
        hidden.reshape(batch * segment, width), whole_head, preferred_element_type=jnp.float32
    ).reshape(batch, segment, vocab_dev)
    refs = ref_logits.astype(jnp.float32)
    local_top = jnp.max(logits, axis=2)
    local_rtop = jnp.max(refs, axis=2)
    top_policy, top_ref = lax.pmax((local_top, local_rtop), "vocab")
    expo = jnp.exp(logits - top_policy[:, :, None])
    total, ref_total, weighted = lax.psum(
        (
            jnp.sum(expo, axis=2),
            jnp.sum(jnp.exp(refs - top_ref[:, :, None]), axis=2),
            jnp.sum(expo * (logits - refs), axis=2),
        ),
        "vocab",
    )
    lse_policy = top_policy + jnp.log(total)
    lse_ref = top_ref + jnp.log(ref_total)
    kl_value = weighted / total - lse_policy + lse_ref
    position = seq_start + lax.broadcasted_iota(jnp.int32, (1, segment), 1)
    live = ((loss_mask == 1) & (position <= end_pos[:, None])).astype(jnp.float32)
    at_end = (position == end_pos[:, None]).astype(jnp.float32)
    reward = -0.01 * kl_value * live + scores[:, None] * at_end
    upper = (
        lax.broadcasted_iota(jnp.int32, (segment, segment), 0)
        >= lax.broadcasted_iota(jnp.int32, (segment, segment), 1)
    ).astype(jnp.float32)
    local_returns = jnp.dot(reward, upper, precision=lax.Precision.HIGHEST)
    totals = jnp.sum(reward, axis=1)
    carried = jnp.zeros_like(totals)
    for _ in range(lax.axis_size("seq") - 1):
        carried = from_behind(totals + carried, "seq", -1)
    returns = local_returns + carried[:, None]
    count, first_moment, second_moment = lax.psum(
        (jnp.sum(live), jnp.sum(live * returns), jnp.sum(live * returns * returns)), "seq"
    )
    count = jnp.maximum(count, 1.0)
    mean = first_moment / count
    var = second_moment / count - mean * mean
    advantages = (returns - mean) / jnp.sqrt(var + 1e-05)
    factor = live * advantages / count
    prob = jnp.exp(logits - lse_policy[:, :, None])
    column = vocab_start + lax.broadcasted_iota(jnp.int32, (1, 1, vocab_dev), 2)
    onehot = (column == token_ids[:, :, None]).astype(jnp.float32)
    logit_grad = (factor[:, :, None] * (prob - onehot)).astype(jnp.bfloat16)
    partial_grad = lax.dot_general(
        logit_grad.reshape(batch * segment, vocab_dev),
        whole_head,
        (((1,), (1,)), ((), ())),
        preferred_element_type=jnp.float32,
    ).reshape(batch, segment, width)
    hidden_grad = lax.psum_scatter(partial_grad, "vocab", scatter_dimension=2, tiled=True).astype(
        jnp.bfloat16
    )
    return (logit_grad, hidden_grad, advantages)


def solution(mesh):
    in_specs = (
        P(None, "seq", None),
        P("seq", "vocab"),
        P(None, "seq", "vocab"),
        P(None, "seq"),
        P(),
        P(None, "seq"),
        P(),
    )
    out_specs = (P(None, "seq", "vocab"), P(None, "seq", "vocab"), P(None, "seq"))
    return jax.shard_map(
        per_device, mesh=mesh, in_specs=in_specs, out_specs=out_specs, check_vma=False
    )
```

profile of v0, /device:TPU:8, one launch (start us, length us, event | category | flops | bytes accessed | tf_op | source)
XLA Modules:
  0.0 593.1 jit_solution(15525419192187923961)
XLA Ops:
  7.2 0.0 copy-start
  7.2 0.0 all-gather.2.cloned.1.call-start
  7.2 0.7 all-gather.2.cloned.1.call-update
  7.9 0.0 reduce-scatter.2.cloned.1.call-start
  8.0 1.5 reduce_max.24
  9.5 124.9 %all-gather.2.cloned.1.call-done = bf16[5120,2432]{1,0:T(8,128)(2,1)} async-done(((bf16[640,2432]{1,0:T(8,128)(2,1)}), bf16[5120,2432]{1,0:T(8,128)(2,1)}) %all-gather.2.cloned.1.call-update) | async-done | bytes 24903696 | tf_op jit(solution)/shard_map/all_gather | solution.py:18
  134.5 0.0 copy-done
  134.5 13.4 %fusion.14 = (f32[2,128]{1,0:T(2,128)S(1)}, f32[2,128,2432]{2,1,0:T(8,128)}) fusion(bf16[2,128,5120]{2,1,0:T(8,128)(2,1)S(1)} %copy-done, bf16[5120,2432]{1,0:T(8,128)(2,1)} %all-gather.2.cloned.1.call-done), kind=kOutput, calls=%fused_computation.28 | convolution fusion | flops 6375964672 | bytes 30016512 | tf_op jit(solution)/shard_map/dot_general | solution.py:19
  147.8 0.0 copy-start.3
  147.8 0.0 copy-start.4
  147.8 0.0 copy-start.5
  147.8 0.0 copy-start.2
  147.8 75.2 %all-reduce.1 = (f32[2,128]{1,0:T(2,128)S(1)}, f32[2,128]{1,0:T(2,128)S(1)}) all-reduce(f32[2,128]{1,0:T(2,128)S(1)} %get-tuple-element.23, bf16[2,128]{1,0:T(2,128)(2,1)S(1)} %reduce_max.24), channel_id=1, replica_groups=mesh['seq'=8,'vocab'=32] {'vocab'}, use_global_device_ids=true, to_apply=%region_1.0 | all-reduce | flops 512 | bytes 3584 | tf_op jit(solution)/shard_map/pmax | solution.py:25
  223.1 3.2 fusion.5
  226.3 69.6 %all-reduce = (f32[2,128]{1,0:T(2,128)S(1)}, f32[2,128]{1,0:T(2,128)S(1)}, f32[2,128]{1,0:T(2,128)S(1)}) all-reduce(f32[2,128]{1,0:T(2,128)S(1)} %get-tuple-element.4, f32[2,128]{1,0:T(2,128)S(1)} %get-tuple-element.5, f32[2,128]{1,0:T(2,128)S(1)} %get-tuple-element.3), channel_id=1, replica_groups=mesh['seq'=8,'vocab'=32] {'vocab'}, use_global_device_ids=true, to_apply=%region_5.0 | all-reduce | flops 768 | bytes 6144 | tf_op jit(solution)/shard_map/psum | solution.py:27
  296.0 0.0 copy-done.3
  296.0 0.0 copy-done.4
  296.0 0.0 copy-done.5
  296.0 0.2 fusion.12
  296.1 1.9 collective-permute-start
  298.1 1.3 collective-permute-done
  299.4 3.6 collective-permute-start.1
  302.9 1.3 collective-permute-done.1
  304.2 3.6 collective-permute-start.2
  307.8 1.3 collective-permute-done.2
  309.1 3.6 collective-permute-start.3
  312.6 1.3 collective-permute-done.3
  313.9 3.6 collective-permute-start.4
  317.5 1.3 collective-permute-done.4
  318.8 3.6 collective-permute-start.5
  322.3 1.3 collective-permute-done.5
  323.6 3.6 collective-permute-start.6
  327.2 1.3 collective-permute-done.6
  328.5 0.8 select_reduce_fusion
  329.2 12.5 %all-reduce.2 = (f32[]{:T(128)}, f32[]{:T(128)}, f32[]{:T(128)}) all-reduce(f32[]{:T(128)} %get-tuple-element.7, f32[]{:T(128)} %get-tuple-element.8, f32[]{:T(128)} %get-tuple-element.6), channel_id=1, replica_groups=mesh['seq'=8,'vocab'=32] {'seq'}, use_global_device_ids=true, to_apply=%region_16.0 | all-reduce | flops 3 | bytes 24 | tf_op jit(solution)/shard_map/psum | solution.py:52
  343.7 0.6 select_divide_fusion
  344.3 0.0 copy-done.2
  344.3 2.5 multiply_convert_fusion
  346.8 0.0 copy-start.1
  346.8 1.0 copy-done.1
  347.9 14.2 %fusion = f32[2,128,5120]{1,2,0:T(8,128)} fusion(bf16[2,128,2432]{2,1,0:T(8,128)(2,1)S(1)} %multiply_convert_fusion, bf16[5120,2432]{1,0:T(8,128)(2,1)} %all-gather.2.cloned.1.call-done), kind=kOutput, calls=%fused_computation | convolution fusion | flops 6375342080 | bytes 31391744 | tf_op jit(solution)/shard_map/dot_general | solution.py:64
  362.0 0.0 reduce-scatter.2.cloned.1.call-update
  362.1 222.7 %reduce-scatter.2.cloned.1.call-done = f32[2,128,160]{1,2,0:T(8,128)} async-done(((f32[2,128,5120]{1,2,0:T(8,128)}), f32[2,128,160]{1,2,0:T(8,128)}) %reduce-scatter.2.cloned.1.call-update) | async-done | bytes 163856 | tf_op jit(solution)/shard_map/reduce_scatter | solution.py:70
  584.7 1.6 convert_element_type.21
  (8 shorter events, 0.0 us)
Async XLA Ops:
  7.2 127.3 %copy-start = (bf16[2,128,5120]{2,1,0:T(8,128)(2,1)S(1)}, bf16[2,128,5120]{2,1,0:T(8,128)(2,1)}, u32[]{:S(2)}) copy-start(bf16[2,128,5120]{2,1,0:T(8,128)(2,1)} %param.7) | copy-start | bytes 7864324
  7.2 127.3 %all-gather.2.cloned.1.call-start = ((), (), s32[]{:S(2)}) async-start(), calls=%async_computation.1 | async-start | bytes 28016640 | tf_op jit(solution)/shard_map/all_gather | solution.py:18
  7.9 576.8 %reduce-scatter.2.cloned.1.call-start = ((), (), s32[]{:S(2)}) async-start(), calls=%async_computation.2 | async-start | bytes 5406720 | tf_op jit(solution)/shard_map/reduce_scatter | solution.py:70
  147.8 148.1 %copy-start.3 = (s32[2,128]{1,0:T(2,128)S(1)}, s32[2,128]{1,0:T(2,128)}, u32[]{:S(2)}) copy-start(s32[2,128]{1,0:T(2,128)} %param.12) | copy-start | bytes 3076
  147.8 148.1 %copy-start.4 = (f32[2]{0:T(128)S(1)}, f32[2]{0:T(128)}, u32[]{:S(2)}) copy-start(f32[2]{0:T(128)} %param.13) | copy-start | bytes 28
  147.8 148.1 %copy-start.5 = (s32[2]{0:T(128)S(1)}, s32[2]{0:T(128)}, u32[]{:S(2)}) copy-start(s32[2]{0:T(128)} %param.11) | copy-start | bytes 28
  147.8 196.5 %copy-start.2 = (s32[2,128]{1,0:T(2,128)S(1)}, s32[2,128]{1,0:T(2,128)}, u32[]{:S(2)}) copy-start(s32[2,128]{1,0:T(2,128)} %param.10) | copy-start | bytes 3076
  296.1 3.2 collective-permute-start
  299.4 4.8 collective-permute-start.1
  304.2 4.8 collective-permute-start.2
  309.1 4.8 collective-permute-start.3
  313.9 4.8 collective-permute-start.4
  318.8 4.8 collective-permute-start.5
  323.6 4.8 collective-permute-start.6
  346.8 1.0 copy-start.1
Sparse Core Ops, SparseCore 0:
  9.8 124.5 all-gather.1
  362.2 222.4 reduce-scatter.1
where the time goes:
time: 594 us; the launch traced here: 593 us
  waiting for transfers between devices  357 us (60%)
  blocking collectives  157 us (26%)
  matrix products  28.3 us (5%)
  starting transfers between devices  23.4 us (4%)
  between operations  16.2 us (3%)
  other arithmetic  9.68 us (2%)
    reduce_scatter x1, waiting for transfers between devices, per_device(): lax.psum_scatter(partial_grad, 'vocab', scatter_dimension=2, tiled=True)  223 us
    all_gather x1, waiting for transfers between devices, per_device(): whole_head = lax.all_gather(head_weight, 'seq', axis=0, tiled=True)  125 us
    pmax x1, blocking collectives, per_device(): top_policy, top_ref = lax.pmax((local_top, local_rtop), 'vocab')  75.2 us
    psum x1, blocking collectives, per_device(): lax.psum((jnp.sum(expo, axis=2), jnp.sum(jnp.exp(refs - top_ref[:, :, Non...  69.6 us
    ppermute x7, starting transfers between devices, from_behind(): return lax.ppermute(shard, axis, pairs)  23.3 us
    dot_general x1, matrix products, per_device(): lax.dot_general(logit_grad.reshape(batch * segment, vocab_dev), whole_hea...  14.2 us
    dot_general x1, matrix products, per_device(): jnp.dot(hidden.reshape(batch * segment, width), whole_head, preferred_ele...  13.4 us
    psum x1, blocking collectives, per_device(): lax.psum((jnp.sum(live), jnp.sum(live * returns), jnp.sum(live * returns...  12.5 us
  transfers between devices with their start and end apart: 9, of which 9 were waited for; matrix products, arithmetic and copies ran while one was open for 0% of the time, Pallas kernels for 0%

commit v1 on v0

--- a/solution.py
+++ b/solution.py
@@ -15,7 +15,11 @@
     vocab_dev = head_weight.shape[1]
     seq_start = lax.axis_index("seq") * segment
     vocab_start = lax.axis_index("vocab") * vocab_dev
-    whole_head = lax.all_gather(head_weight, "seq", axis=0, tiled=True)
+    size = lax.axis_size("seq")
+    repeats = [size if d == 0 else 1 for d in range(head_weight.ndim)]
+    whole_head = lax.all_to_all(
+        jnp.tile(head_weight, repeats), "seq", split_axis=0, concat_axis=0, tiled=True
+    )
     logits = jnp.dot(
         hidden.reshape(batch * segment, width), whole_head, preferred_element_type=jnp.float32
     ).reshape(batch, segment, vocab_dev)

time: 594 us -> 760 us (1.28)
  waiting for transfers between devices: 357 us -> 499 us
  local copies, waits for them, and re-layouts: 1.05 us -> 15.8 us
  starting transfers between devices: 23.4 us -> 31.8 us
    all_to_all x0 -> x1, waiting for transfers between devices: none -> 269 us  [per_device(): lax.all_to_all(jnp.tile(head_weight, repeats), 'seq', split_axis=0, conca...]
    all_gather x1 -> x0, waiting for transfers between devices: 125 us -> none  [per_device(): whole_head = lax.all_gather(head_weight, 'seq', axis=0, tiled=True)]
    another operation x0 -> x1, local copies, waits for them, and re-layouts: none -> 14.7 us  [per_device(): jnp.tile(head_weight, repeats)]
    all_to_all x0 -> x1, starting transfers between devices: none -> 8.49 us  [per_device(): lax.all_to_all(jnp.tile(head_weight, repeats), 'seq', split_axis=0, conca...]
where the time goes in v1:
time: 760 us; the launch traced here: 759 us
  waiting for transfers between devices  499 us (66%)
  blocking collectives  158 us (21%)
  starting transfers between devices  31.8 us (4%)
  matrix products  28.3 us (4%)
  between operations  16.1 us (2%)
  local copies, waits for them, and re-layouts  15.8 us (2%)
  other arithmetic  9.68 us (1%)
    all_to_all x1, waiting for transfers between devices, per_device(): lax.all_to_all(jnp.tile(head_weight, repeats), 'seq', split_axis=0, conca...  269 us
    reduce_scatter x1, waiting for transfers between devices, per_device(): lax.psum_scatter(partial_grad, 'vocab', scatter_dimension=2, tiled=True)  221 us
    pmax x1, blocking collectives, per_device(): top_policy, top_ref = lax.pmax((local_top, local_rtop), 'vocab')  76.1 us
    psum x1, blocking collectives, per_device(): lax.psum((jnp.sum(expo, axis=2), jnp.sum(jnp.exp(refs - top_ref[:, :, Non...  69.6 us
    ppermute x7, starting transfers between devices, from_behind(): return lax.ppermute(shard, axis, pairs)  23.3 us
  transfers between devices with their start and end apart: 9, of which 9 were waited for; matrix products, arithmetic and copies ran while one was open for 0% of the time, Pallas kernels for 0%

profile of v1, /device:TPU:8, one launch (start us, length us, event | category | flops | bytes accessed | tf_op | source)
XLA Modules:
  0.0 758.7 jit_solution(6258219236786466544)
XLA Ops:
  7.2 0.0 copy-start
  7.2 14.7 %tile.2 = bf16[8,640,2432]{2,1,0:T(8,128)(2,1)} broadcast(bf16[640,2432]{1,0:T(8,128)(2,1)} %param.8), dimensions={1,2} | broadcast | bytes 28016640 | tf_op jit(solution)/shard_map/tile | solution.py:21
  21.9 8.5 %all-to-all-start = ((bf16[8,640,2432]{2,1,0:T(8,128)(2,1)}), bf16[8,640,2432]{2,1,0:T(8,128)(2,1)}, u32[]{:S(2)}, u32[]{:S(2)}) async-start(bf16[8,640,2432]{2,1,0:T(8,128)(2,1)} %tile.2), calls=%async_computation | async-start | bytes 49807360 | tf_op jit(solution)/shard_map/all_to_all | solution.py:20
  30.4 0.0 reduce-scatter.2.cloned.1.call-start
  30.4 1.5 reduce_max.24
  31.9 268.7 %all-to-all-done = bf16[8,640,2432]{2,1,0:T(8,128)(2,1)} async-done(((bf16[8,640,2432]{2,1,0:T(8,128)(2,1)}), bf16[8,640,2432]{2,1,0:T(8,128)(2,1)}, u32[]{:S(2)}, u32[]{:S(2)}) %all-to-all-start) | async-done | bytes 24903712 | tf_op jit(solution)/shard_map/all_to_all | solution.py:20
  300.6 0.0 copy-done
  300.6 13.4 %fusion.10 = (f32[2,128]{1,0:T(2,128)S(1)}, f32[2,128,2432]{2,1,0:T(8,128)}) fusion(bf16[2,128,5120]{2,1,0:T(8,128)(2,1)S(1)} %copy-done, bf16[5120,2432,1]{1,0,2:T(8,128)(2,1)} %bitcast.1), kind=kOutput, calls=%fused_computation.24 | convolution fusion | flops 6375964672 | bytes 30016512 | tf_op jit(solution)/shard_map/dot_general | solution.py:23
  314.0 0.0 copy-start.3
  314.0 0.0 copy-start.4
  314.0 0.0 copy-start.5
  314.0 0.0 copy-start.2
  314.0 76.1 %all-reduce.1 = (f32[2,128]{1,0:T(2,128)S(1)}, f32[2,128]{1,0:T(2,128)S(1)}) all-reduce(f32[2,128]{1,0:T(2,128)S(1)} %get-tuple-element.23, bf16[2,128]{1,0:T(2,128)(2,1)S(1)} %reduce_max.24), channel_id=1, replica_groups=mesh['seq'=8,'vocab'=32] {'vocab'}, use_global_device_ids=true, to_apply=%region_1.0 | all-reduce | flops 512 | bytes 3584 | tf_op jit(solution)/shard_map/pmax | solution.py:29
  390.1 3.2 fusion.1
  393.3 69.6 %all-reduce = (f32[2,128]{1,0:T(2,128)S(1)}, f32[2,128]{1,0:T(2,128)S(1)}, f32[2,128]{1,0:T(2,128)S(1)}) all-reduce(f32[2,128]{1,0:T(2,128)S(1)} %get-tuple-element.4, f32[2,128]{1,0:T(2,128)S(1)} %get-tuple-element.5, f32[2,128]{1,0:T(2,128)S(1)} %get-tuple-element.3), channel_id=1, replica_groups=mesh['seq'=8,'vocab'=32] {'vocab'}, use_global_device_ids=true, to_apply=%region_5.0 | all-reduce | flops 768 | bytes 6144 | tf_op jit(solution)/shard_map/psum | solution.py:31
  463.0 0.0 copy-done.3
  463.0 0.0 copy-done.4
  463.0 0.0 copy-done.5
  463.0 0.2 fusion.8
  463.2 1.9 collective-permute-start
  465.1 1.3 collective-permute-done
  466.4 3.6 collective-permute-start.1
  469.9 1.3 collective-permute-done.1
  471.2 3.6 collective-permute-start.2
  474.8 1.3 collective-permute-done.2
  476.1 3.6 collective-permute-start.3
  479.6 1.3 collective-permute-done.3
  480.9 3.6 collective-permute-start.4
  484.5 1.3 collective-permute-done.4
  485.8 3.6 collective-permute-start.5
  489.3 1.3 collective-permute-done.5
  490.6 3.6 collective-permute-start.6
  494.2 1.3 collective-permute-done.6
  495.5 0.8 select_reduce_fusion
  496.2 12.5 %all-reduce.2 = (f32[]{:T(128)}, f32[]{:T(128)}, f32[]{:T(128)}) all-reduce(f32[]{:T(128)} %get-tuple-element.7, f32[]{:T(128)} %get-tuple-element.8, f32[]{:T(128)} %get-tuple-element.6), channel_id=1, replica_groups=mesh['seq'=8,'vocab'=32] {'seq'}, use_global_device_ids=true, to_apply=%region_16.0 | all-reduce | flops 3 | bytes 24 | tf_op jit(solution)/shard_map/psum | solution.py:56
  510.7 0.6 select_divide_fusion
  511.4 0.0 copy-done.2
  511.4 2.5 multiply_convert_fusion
  513.9 0.0 copy-start.1
  513.9 1.0 copy-done.1
  514.9 14.2 %fusion.11 = f32[2,128,5120]{1,2,0:T(8,128)} fusion(bf16[2,128,2432]{2,1,0:T(8,128)(2,1)S(1)} %multiply_convert_fusion, bf16[5120,2432,1]{1,0,2:T(8,128)(2,1)} %bitcast.1), kind=kOutput, calls=%fused_computation.25 | convolution fusion | flops 6375342080 | bytes 31391744 | tf_op jit(solution)/shard_map/dot_general | solution.py:68
  529.1 0.0 reduce-scatter.2.cloned.1.call-update
  529.1 221.2 %reduce-scatter.2.cloned.1.call-done = f32[2,128,160]{1,2,0:T(8,128)} async-done(((f32[2,128,5120]{1,2,0:T(8,128)}), f32[2,128,160]{1,2,0:T(8,128)}) %reduce-scatter.2.cloned.1.call-update) | async-done | bytes 163856 | tf_op jit(solution)/shard_map/reduce_scatter | solution.py:74
  750.3 1.6 convert_element_type.21
  (8 shorter events, 0.0 us)
Async XLA Ops:
  7.2 293.5 %copy-start = (bf16[2,128,5120]{2,1,0:T(8,128)(2,1)S(1)}, bf16[2,128,5120]{2,1,0:T(8,128)(2,1)}, u32[]{:S(2)}) copy-start(bf16[2,128,5120]{2,1,0:T(8,128)(2,1)} %param.7) | copy-start | bytes 7864324
  21.9 278.7 %all-to-all-start = ((bf16[8,640,2432]{2,1,0:T(8,128)(2,1)}), bf16[8,640,2432]{2,1,0:T(8,128)(2,1)}, u32[]{:S(2)}, u32[]{:S(2)}) async-start(bf16[8,640,2432]{2,1,0:T(8,128)(2,1)} %tile.2), calls=%async_computation | async-start | bytes 49807360 | tf_op jit(solution)/shard_map/all_to_all | solution.py:20
  30.4 719.9 %reduce-scatter.2.cloned.1.call-start = ((), (), s32[]{:S(2)}) async-start(), calls=%async_computation.2 | async-start | bytes 5406720 | tf_op jit(solution)/shard_map/reduce_scatter | solution.py:74
  314.0 149.0 %copy-start.3 = (s32[2,128]{1,0:T(2,128)S(1)}, s32[2,128]{1,0:T(2,128)}, u32[]{:S(2)}) copy-start(s32[2,128]{1,0:T(2,128)} %param.12) | copy-start | bytes 3076
  314.0 149.0 %copy-start.4 = (f32[2]{0:T(128)S(1)}, f32[2]{0:T(128)}, u32[]{:S(2)}) copy-start(f32[2]{0:T(128)} %param.13) | copy-start | bytes 28
  314.0 149.0 %copy-start.5 = (s32[2]{0:T(128)S(1)}, s32[2]{0:T(128)}, u32[]{:S(2)}) copy-start(s32[2]{0:T(128)} %param.11) | copy-start | bytes 28
  314.0 197.4 %copy-start.2 = (s32[2,128]{1,0:T(2,128)S(1)}, s32[2,128]{1,0:T(2,128)}, u32[]{:S(2)}) copy-start(s32[2,128]{1,0:T(2,128)} %param.10) | copy-start | bytes 3076
  463.2 3.2 collective-permute-start
  466.4 4.8 collective-permute-start.1
  471.2 4.8 collective-permute-start.2
  476.1 4.8 collective-permute-start.3
  480.9 4.8 collective-permute-start.4
  485.8 4.8 collective-permute-start.5
  490.6 4.8 collective-permute-start.6
  513.9 1.0 copy-start.1
Sparse Core Ops, SparseCore 0:
  529.2 221.0 reduce-scatter.1
